TPU v7x, 128 devices: a whole 4x4x4 slice. The times are simulated.
128 devices in a mesh: row: 16 (over y, x), col: 4 (over z), dp: 2 (over core).
Axes of the slice: x: 4, y: 4, z: 4, core: 2. Of those that a mesh axis runs over, the one named last changes fastest.
Arguments:
- inputs: bfloat16 [1024, 8192], P(('col', 'dp'), 'row'), may hold values from -6 to 6
- gate_weight: bfloat16 [8192, 14336], P('row', 'col'), may hold values from -0.0625 to 0.0625
- up_weight: bfloat16 [8192, 14336], P('row', 'col'), may hold values from -0.0625 to 0.0625
- down_weight: bfloat16 [14336, 8192], P('col', 'row'), may hold values from -0.046875 to 0.046875
- reward_head: bfloat16 [8192], P('row'), may hold values from -0.0625 to 0.0625
- upstream: bfloat16 [1024, 8192], P(('col', 'dp'), 'row'), may hold values from -0.59765625 to 0.59765625
- labels: int32 [1024], P(('col', 'dp')), may hold values from 0 to 1
- label_mask: int32 [1024], P(('col', 'dp')), may hold values 0 or 1
Outputs:
- gate_grad: float32 [8192, 14336], P(('row', 'dp'), 'col')
- up_grad: float32 [8192, 14336], P(('row', 'dp'), 'col')
- down_grad: float32 [14336, 8192], P(('col', 'dp'), 'row')
- input_grad: float32 [1024, 8192], P(('col', 'dp'), 'row')
All inputs are finite; a program needn't handle non-finite values. No bound on the sum of `label_mask` on one device may be relied on, other than what follows from the above.
Results may differ from a plain program's by a relative error of at most 0.035.
Values may be sent and summed in bfloat16 or wider, within the bound.
No kernel may reach another device: no remote copies, remote signals or barrier semaphores. Data moves between devices by JAX's collectives and lax.ppermute only.
A program may use at most 128 MiB of HBM per device.

v0:
```python
import jax
import jax.numpy as jnp
from jax import lax
from jax.sharding import PartitionSpec as P

reward_weight = 8.0
BF = jnp.bfloat16
F32 = jnp.float32


def transpose_product(left, right):
    return lax.dot_general(left, right, (((0,), (0,)), ((), ())), preferred_element_type=F32)


def right_transpose(left, right):
    return lax.dot_general(left, right, (((1,), (1,)), ((), ())), preferred_element_type=F32)


def per_device(
    inputs, gate_weight, up_weight, down_weight, reward_head, upstream, labels, label_mask
):
    tokens, depth = inputs.shape
    half = gate_weight.shape[1] // 2
    n_row = lax.axis_size("row")
    core = lax.axis_index("dp")
    row = lax.axis_index("row")
    token_axes = ("col", "dp")
    tags = jnp.stack([labels, label_mask], axis=1).astype(BF)
    tags = jnp.pad(tags, ((0, 0), (0, 126)))
    packed = jnp.concatenate([inputs, upstream, tags], axis=1)
    everyone = lax.all_gather(packed, token_axes, axis=0, tiled=True)
    x_all = everyone[:, :depth]
    upstream_all = everyone[:, depth : 2 * depth]
    total = x_all.shape[0]
    mine = total // n_row
    gate_half = lax.dynamic_slice_in_dim(gate_weight, core * half, half, 1)
    up_half = lax.dynamic_slice_in_dim(up_weight, core * half, half, 1)
    down_half = lax.dynamic_slice_in_dim(down_weight, core * half, half, 0)
    head_value = reward_head.astype(F32)
    head_hidden = jnp.dot(down_half.astype(F32), head_value, precision=lax.Precision.HIGHEST)
    head_inputs = jnp.dot(x_all.astype(F32), head_value, precision=lax.Precision.HIGHEST)
    per_token = half // mine
    extras = jnp.concatenate(
        [
            head_inputs[:, None],
            jnp.tile(head_hidden.reshape(mine, per_token), (n_row, 1)),
            jnp.zeros((total, 127 - per_token), F32),
        ],
        axis=1,
    )
    partial = jnp.concatenate(
        [
            jnp.dot(x_all, gate_half, preferred_element_type=F32).astype(BF),
            jnp.dot(x_all, up_half, preferred_element_type=F32).astype(BF),
            right_transpose(upstream_all, down_half).astype(BF),
            extras.astype(BF),
        ],
        axis=1,
    )
    summed = lax.psum_scatter(partial, "row", scatter_dimension=0, tiled=True).astype(F32)
    gate = summed[:, :half]
    upper = summed[:, half : 2 * half]
    grad_upstream = summed[:, 2 * half : 3 * half]
    extra = summed[:, 3 * half :]
    head_hidden = extra[:, 1 : 1 + per_token].reshape(half)
    sigmoid_gate = jax.nn.sigmoid(gate)
    hidden = (gate * sigmoid_gate * upper).astype(BF)
    score = extra[:, 0] + lax.psum(
        jnp.sum(hidden.astype(F32) * head_hidden[None, :], axis=1), token_axes
    )
    own_tags = lax.dynamic_slice_in_dim(everyone[:, 2 * depth :], row * mine, mine, 0).astype(F32)
    slope = reward_weight * own_tags[:, 1] * (jax.nn.sigmoid(score) - own_tags[:, 0])
    grad_hidden = grad_upstream + slope[:, None] * head_hidden[None, :]
    grad_gate = (grad_hidden * upper * sigmoid_gate * (1.0 + gate * (1.0 - sigmoid_gate))).astype(
        BF
    )
    grad_upper = (grad_hidden * gate * sigmoid_gate).astype(BF)
    slope_high = slope.astype(BF)
    slope_low = (slope - slope_high.astype(F32)).astype(BF)
    slopes = jnp.pad(jnp.stack([slope_high, slope_low], axis=1), ((0, 0), (0, 126)))
    gathered = lax.all_gather(
        jnp.concatenate([hidden, grad_gate, grad_upper, slopes], axis=1), "row", axis=0, tiled=True
    )
    hidden_all = gathered[:, :half]
    grad_gate_all = gathered[:, half : 2 * half]
    grad_upper_all = gathered[:, 2 * half : 3 * half]
    slope_all = gathered[:, 3 * half].astype(F32) + gathered[:, 3 * half + 1].astype(F32)
    input_part = right_transpose(grad_gate_all, gate_half) + right_transpose(
        grad_upper_all, up_half
    )
    input_sum = lax.psum_scatter(
        input_part.astype(BF), token_axes, scatter_dimension=0, tiled=True
    ).astype(F32)
    place = (lax.axis_index("col") * 2 + core) * tokens
    own_slope = lax.dynamic_slice_in_dim(slope_all, place, tokens, 0)
    input_grad = upstream.astype(F32) + own_slope[:, None] * head_value[None, :] + input_sum
    grad_mixed = (upstream_all.astype(F32) + slope_all[:, None] * head_value[None, :]).astype(BF)
    down_grad = transpose_product(hidden_all, grad_mixed)

    def both_halves(part):
        keep = lax.dynamic_slice_in_dim(part, core * (depth // 2), depth // 2, 0)
        send = lax.dynamic_slice_in_dim(part, (1 - core) * (depth // 2), depth // 2, 0)
        other = lax.ppermute(send.astype(BF), "dp", [(0, 1), (1, 0)]).astype(F32)
        first = core == 0
        return jnp.concatenate(
            [jnp.where(first, keep, other), jnp.where(first, other, keep)], axis=1
        )

    gate_grad = both_halves(transpose_product(x_all, grad_gate_all))
    up_grad = both_halves(transpose_product(x_all, grad_upper_all))
    return (gate_grad, up_grad, down_grad, input_grad)


def solution(mesh):
    in_specs = (
        P(("col", "dp"), "row"),
        P("row", "col"),
        P("row", "col"),
        P("col", "row"),
        P("row"),
        P(("col", "dp"), "row"),
        P(("col", "dp")),
        P(("col", "dp")),
    )
    out_specs = (
        P(("row", "dp"), "col"),
        P(("row", "dp"), "col"),
        P(("col", "dp"), "row"),
        P(("col", "dp"), "row"),
    )
    return jax.shard_map(
        per_device, mesh=mesh, in_specs=in_specs, out_specs=out_specs, check_vma=False
    )
```

profile of v0, /device:TPU:0, one launch (start us, length us, event | category | flops | bytes accessed | tf_op | source)
XLA Modules:
  0.0 312.7 jit_solution(9628465307973189131)
XLA Ops:
  7.2 0.7 convert_bitcast_fusion.2
  8.0 1.7 fusion.37
  9.8 0.7 reshape.23
  10.5 2.1 fusion.22
  12.7 25.9 %all-gather.3.cloned.1.call-done = bf16[1024,1152]{1,0:T(8,128)(2,1)} async-done(((bf16[128,1152]{1,0:T(8,128)(2,1)}), bf16[1024,1152]{1,0:T(8,128)(2,1)}) %all-gather.3.cloned.1.call-update) | async-done | bytes 2359312 | tf_op jit(solution)/shard_map/all_gather | solution.py:31
  38.6 1.6 fusion.33
  40.4 5.9 %convolution_convert_fusion = bf16[1024,1792]{1,0:T(8,128)(2,1)} fusion(bf16[3584,512]{1,0:T(8,128)(2,1)} %param.11, s32[]{:T(128)S(6)} %select_n.40, bf16[1024,1152]{1,0:T(8,128)(2,1)} %all-gather.3.cloned.1.call-done), kind=kOutput, calls=%fused_computation | convolution fusion | flops 1880883200 | bytes 6553604 | tf_op jit(solution)/shard_map/dot_general | solution.py:16
  46.4 3.9 %convolution_convert_fusion.1 = bf16[1024,1792]{1,0:T(8,128)(2,1)} fusion(bf16[512,3584]{1,0:T(8,128)(2,1)S(1)} %copy-done.4, s32[]{:T(128)S(6)} %select_n.40, bf16[1024,1152]{1,0:T(8,128)(2,1)S(1)} %copy-done), kind=kOutput, calls=%fused_computation.1 | convolution fusion | flops 1880883200 | bytes 6553604 | tf_op jit(solution)/shard_map/dot_general | solution.py:54
  50.3 3.9 %convolution_convert_fusion.2 = bf16[1024,1792]{1,0:T(8,128)(2,1)} fusion(bf16[512,3584]{1,0:T(8,128)(2,1)S(1)} %copy-done.5, s32[]{:T(128)S(6)} %select_n.40, bf16[1024,1152]{1,0:T(8,128)(2,1)S(1)} %copy-done), kind=kOutput, calls=%fused_computation.2 | convolution fusion | flops 1880883200 | bytes 6553604 | tf_op jit(solution)/shard_map/dot_general | solution.py:53
  54.3 18.4 %concatenate.19 = bf16[1024,5504]{1,0:T(8,128)(2,1)} concatenate(bf16[1024,1792]{1,0:T(8,128)(2,1)} %convolution_convert_fusion.2, bf16[1024,1792]{1,0:T(8,128)(2,1)} %convolution_convert_fusion.1, bf16[1024,1792]{1,0:T(8,128)(2,1)} %convolution_convert_fusion, bf16[1024,1]{1,0:T(8,128)(2,1)S(1)} %broadcast_in_dim.14, bf16[1024,28]{1,0:T(8,128)(2,1)S(1)} %bitcast.12, ...), dimensions={1} | concatenate | bytes 22544384 | tf_op jit(solution)/shard_map/concatenate | solution.py:51
  72.7 0.9 slice-done
  73.8 90.5 %reduce-scatter.3.cloned.1.call-done = bf16[64,5504]{1,0:T(8,128)(2,1)} async-done(((bf16[1024,5504]{1,0:T(8,128)(2,1)}), bf16[64,5504]{1,0:T(8,128)(2,1)}) %reduce-scatter.3.cloned.1.call-update) | async-done | bytes 704528 | tf_op jit(solution)/shard_map/reduce_scatter | solution.py:60
  164.3 0.8 slice.71
  165.2 1.2 convert_element_type.87
  166.5 0.2 multiply_reduce_fusion
  166.8 14.2 %psum.7 = f32[64]{0:T(128)S(1)} all-reduce(f32[64]{0:T(128)S(1)} %get-tuple-element.8), channel_id=1, replica_groups=mesh['row'=16,'col'=4,'dp'=2] {'col','dp'}, use_global_device_ids=true, to_apply=%region_2.3 | all-reduce | flops 64 | bytes 512 | tf_op jit(solution)/shard_map/psum | solution.py:68
  181.0 0.3 multiply_convert_fusion.1
  181.4 0.9 fusion.29
  182.4 80.0 %all-gather.5.cloned.1.call-done = bf16[1024,5504]{1,0:T(8,128)(2,1)} async-done(((bf16[64,5504]{1,0:T(8,128)(2,1)}), bf16[1024,5504]{1,0:T(8,128)(2,1)}) %all-gather.5.cloned.1.call-update) | async-done | bytes 11272208 | tf_op jit(solution)/shard_map/all_gather | solution.py:81
  262.4 4.8 %fusion.2 = f32[1024,512]{1,0:T(8,128)S(1)} fusion(bf16[1024,5504]{1,0:T(8,128)(2,1)} %all-gather.5.cloned.1.call-done, bf16[512,3584]{1,0:T(8,128)(2,1)} %param.10, s32[]{:T(128)S(6)} %select_n.40), kind=kOutput, calls=%fused_computation.7 | convolution fusion | flops 1879048192 | bytes 7602180 | tf_op jit(solution)/shard_map/dot_general | solution.py:16
  267.3 5.2 %add_convert_fusion = bf16[1024,512]{1,0:T(8,128)(2,1)} fusion(f32[1024,512]{1,0:T(8,128)S(1)} %fusion.2, bf16[512,3584]{1,0:T(8,128)(2,1)S(1)} %copy-done.6, s32[]{:T(128)S(6)} %select_n.40, bf16[1024,5504]{1,0:T(8,128)(2,1)} %all-gather.5.cloned.1.call-done), kind=kOutput, calls=%fused_computation.19 | convolution fusion | flops 1880096768 | bytes 8650756 | tf_op jit(solution)/shard_map/dot_general | solution.py:16
  272.5 4.2 %fusion.4 = f32[512,1792]{1,0:T(8,128)S(1)} fusion(bf16[1024,5504]{1,0:T(8,128)(2,1)} %all-gather.5.cloned.1.call-done, bf16[1024,1152]{1,0:T(8,128)(2,1)S(1)} %copy-done.1), kind=kOutput, calls=%fused_computation.9 | convolution fusion | flops 1879048192 | bytes 8388608 | tf_op jit(solution)/shard_map/dot_general | solution.py:12
  276.8 0.3 collective-permute-start.1
  277.1 4.1 %fusion.8 = f32[512,1792]{1,0:T(8,128)S(1)} fusion(bf16[1024,5504]{1,0:T(8,128)(2,1)} %all-gather.5.cloned.1.call-done, bf16[1024,1152]{1,0:T(8,128)(2,1)S(1)} %copy-done.1), kind=kOutput, calls=%fused_computation.13 | convolution fusion | flops 1879048192 | bytes 8388608 | tf_op jit(solution)/shard_map/dot_general | solution.py:12
  281.3 0.6 collective-permute-start
  281.9 1.5 convert_add_fusion
  283.6 6.1 %fusion = f32[1792,512]{1,0:T(8,128)} fusion(bf16[1024,5504]{1,0:T(8,128)(2,1)} %all-gather.5.cloned.1.call-done, f32[512]{0:T(512)S(1)} %convert_element_type.103, f32[1024]{0:T(1024)S(1)} %get-tuple-element.11, bf16[1024,1152]{1,0:T(8,128)(2,1)S(1)} %copy-done.1), kind=kOutput, calls=%fused_computation.3 | convolution fusion | flops 1881145344 | bytes 8394752 | tf_op jit(solution)/shard_map/dot_general | solution.py:12
  289.6 0.3 convert_select_fusion.1
  289.9 2.3 pad_maximum_fusion.1
  292.5 2.3 pad_maximum_fusion
  294.8 9.6 %reduce-scatter.5.cloned.1.call-done = bf16[128,512]{1,0:T(8,128)(2,1)} async-done(((bf16[1024,512]{1,0:T(8,128)(2,1)}), bf16[128,512]{1,0:T(8,128)(2,1)}) %reduce-scatter.5.cloned.1.call-update) | async-done | bytes 131088 | tf_op jit(solution)/shard_map/reduce_scatter | solution.py:91
  304.4 1.7 convert_add_fusion.1
  (45 shorter events, 1.9 us)
Async XLA Ops:
  7.2 31.4 %all-gather.3.cloned.1.call-start = ((), (), s32[]{:S(2)}) async-start(), calls=%async_computation.2 | async-start | bytes 2654208 | tf_op jit(solution)/shard_map/all_gather | solution.py:31
  9.8 154.5 %reduce-scatter.3.cloned.1.call-start = ((), (), s32[]{:S(2)}) async-start(), calls=%async_computation.3 | async-start | bytes 11976704 | tf_op jit(solution)/shard_map/reduce_scatter | solution.py:60
  40.4 5.9 %copy-start = (bf16[1024,1152]{1,0:T(8,128)(2,1)S(1)}, bf16[1024,1152]{1,0:T(8,128)(2,1)}, u32[]{:S(2)}) copy-start(bf16[1024,1152]{1,0:T(8,128)(2,1)} %all-gather.3.cloned.1.call-done) | copy-start | bytes 7077892
  40.4 5.9 %copy-start.4 = (bf16[512,3584]{1,0:T(8,128)(2,1)S(1)}, bf16[512,3584]{1,0:T(8,128)(2,1)}, u32[]{:S(2)}) copy-start(bf16[512,3584]{1,0:T(8,128)(2,1)} %param.10) | copy-start | bytes 11010052
  46.4 3.9 %copy-start.5 = (bf16[512,3584]{1,0:T(8,128)(2,1)S(1)}, bf16[512,3584]{1,0:T(8,128)(2,1)}, u32[]{:S(2)}) copy-start(bf16[512,3584]{1,0:T(8,128)(2,1)} %param.9) | copy-start | bytes 11010052
  72.6 0.9 slice-start
  72.7 189.7 %all-gather.5.cloned.1.call-start = ((), (), s32[]{:S(2)}) async-start(), calls=%async_computation.4 | async-start | bytes 11976704 | tf_op jit(solution)/shard_map/all_gather | solution.py:81
  166.5 15.9 %copy-start.3 = (bf16[512]{0:T(512)(128)(2,1)S(1)}, bf16[512]{0:T(512)(128)(2,1)}, u32[]{:S(2)}) copy-start(bf16[512]{0:T(512)(128)(2,1)} %param.12) | copy-start | bytes 3076
  182.3 122.1 %reduce-scatter.5.cloned.1.call-start = ((), (), s32[]{:S(2)}) async-start(), calls=%async_computation.5 | async-start | bytes 1179648 | tf_op jit(solution)/shard_map/reduce_scatter | solution.py:91
  262.4 4.9 %copy-start.6 = (bf16[512,3584]{1,0:T(8,128)(2,1)S(1)}, bf16[512,3584]{1,0:T(8,128)(2,1)}, u32[]{:S(2)}) copy-start(bf16[512,3584]{1,0:T(8,128)(2,1)} %param.9) | copy-start | bytes 11010052
  267.2 5.3 %copy-start.1 = (bf16[1024,1152]{1,0:T(8,128)(2,1)S(1)}, bf16[1024,1152]{1,0:T(8,128)(2,1)}, u32[]{:S(2)}) copy-start(bf16[1024,1152]{1,0:T(8,128)(2,1)} %all-gather.3.cloned.1.call-done) | copy-start | bytes 7077892
  276.8 12.8 %collective-permute-start.1 = (bf16[256,1792]{1,0:T(8,128)(2,1)S(1)}, bf16[256,1792]{1,0:T(8,128)(2,1)S(1)}, u32[]{:S(2)}, u32[]{:S(2)}) collective-permute-start(bf16[256,1792]{1,0:T(8,128)(2,1)S(1)} %dynamic-slice_convert_fusion), channel_id=1, source_target_pairs={{0,1},{1,0},{2,3},{3,2},{4,5},{5,4},{6,7},{7,6},{8,9},{9,8},{10,11... | collective-permute-start | bytes 2752520 | tf_op jit(solution)/shard_map/ppermute | solution.py:103
  281.3 10.9 %collective-permute-start = (bf16[256,1792]{1,0:T(8,128)(2,1)S(1)}, bf16[256,1792]{1,0:T(8,128)(2,1)S(1)}, u32[]{:S(2)}, u32[]{:S(2)}) collective-permute-start(bf16[256,1792]{1,0:T(8,128)(2,1)S(1)} %dynamic-slice_convert_fusion.1), channel_id=1, source_target_pairs={{0,1},{1,0},{2,3},{3,2},{4,5},{5,4},{6,7},{7,6},{8,9},{9,8},{10,11... | collective-permute-start | bytes 2752520 | tf_op jit(solution)/shard_map/ppermute | solution.py:103
  292.5 12.0 %copy-start.2 = (bf16[128,512]{1,0:T(8,128)(2,1)S(1)}, bf16[128,512]{1,0:T(8,128)(2,1)}, u32[]{:S(2)}) copy-start(bf16[128,512]{1,0:T(8,128)(2,1)} %param.13) | copy-start | bytes 393220
Sparse Core Ops, SparseCore 0:
  10.3 28.2 all-gather.2
  72.8 91.4 reduce-scatter.2
  182.4 79.9 all-gather.4
  272.6 31.7 reduce-scatter.4
where the time goes:
time: 314 us; the launch traced here: 313 us
  waiting for transfers between devices  206 us (66%)
  matrix products  41.9 us (13%)
  local copies, waits for them, and re-layouts  21.9 us (7%)
  blocking collectives  14.2 us (5%)
  between operations  14 us (4%)
  other arithmetic  13.6 us (4%)
    reduce_scatter x1, waiting for transfers between devices, per_device(): lax.psum_scatter(partial, 'row', scatter_dimension=0, tiled=True)  90.5 us
    all_gather x1, waiting for transfers between devices, per_device(): lax.all_gather(jnp.concatenate([hidden, grad_gate, grad_upper, slopes], a...  80 us
    all_gather x1, waiting for transfers between devices, per_device(): everyone = lax.all_gather(packed, token_axes, axis=0, tiled=True)  25.9 us
    concatenate x1, local copies, waits for them, and re-layouts, per_device(): jnp.concatenate([jnp.dot(x_all, gate_half, preferred_element_type=F32).as...  18.4 us
    dot_general x3, matrix products, right_transpose(): lax.dot_general(left, right, (((1,), (1,)), ((), ())), preferred_element_...  16 us
    dot_general x3, matrix products, transpose_product(): lax.dot_general(left, right, (((0,), (0,)), ((), ())), preferred_element_...  14.4 us
    psum x1, blocking collectives, per_device(): lax.psum(jnp.sum(hidden.astype(F32) * head_hidden[None, :], axis=1), toke...  14.2 us
    reduce_scatter x1, waiting for transfers between devices, per_device(): lax.psum_scatter(input_part.astype(BF), token_axes, scatter_dimension=0,...  9.63 us
  transfers between devices with their start and end apart: 6, of which 4 were waited for; matrix products, arithmetic and copies ran while one was open for 8% of the time, Pallas kernels for 0%

commit v1 on v0

--- a/solution.py
+++ b/solution.py
@@ -65,7 +65,8 @@
     head_hidden = extra[:, 1 : 1 + per_token].reshape(half)
     sigmoid_gate = jax.nn.sigmoid(gate)
     hidden = (gate * sigmoid_gate * upper).astype(BF)
-    score = extra[:, 0] + lax.psum(
+    lots_all_assign = lambda target, comm_axis: jnp.sum(lax.all_gather(target, comm_axis), axis=0)
+    score = extra[:, 0] + lots_all_assign(
         jnp.sum(hidden.astype(F32) * head_hidden[None, :], axis=1), token_axes
     )
     own_tags = lax.dynamic_slice_in_dim(everyone[:, 2 * depth :], row * mine, mine, 0).astype(F32)

time: 314 us -> 323 us (1.029)
  local copies, waits for them, and re-layouts: 21.9 us -> 28.5 us
    reduce_scatter x1 -> x0, waiting for transfers between devices: 90.5 us -> none  [per_device(): lax.psum_scatter(partial, 'row', scatter_dimension=0, tiled=True)]
    unnamed x4 -> x5, waiting for transfers between devices: 0.07 us -> 89.9 us
    unnamed x0 -> x1, blocking collectives: none -> 14.2 us
    psum x1 -> x0, blocking collectives: 14.2 us -> none  [per_device(): lax.psum(jnp.sum(hidden.astype(F32) * head_hidden[None, :], axis=1), toke...]
    unnamed x16 -> x25, local copies, waits for them, and re-layouts: 0.86 us -> 7.34 us
where the time goes in v1:
time: 323 us; the launch traced here: 322 us
  waiting for transfers between devices  208 us (64%)
  matrix products  41.8 us (13%)
  local copies, waits for them, and re-layouts  28.5 us (9%)
  between operations  14.7 us (5%)
  blocking collectives  14.2 us (4%)
  other arithmetic  13.9 us (4%)
    unnamed x5, waiting for transfers between devices  89.9 us
    all_gather x1, waiting for transfers between devices, per_device(): lax.all_gather(jnp.concatenate([hidden, grad_gate, grad_upper, slopes], a...  79.7 us
    all_gather x1, waiting for transfers between devices, per_device(): everyone = lax.all_gather(packed, token_axes, axis=0, tiled=True)  28.2 us
    concatenate x1, local copies, waits for them, and re-layouts, per_device(): jnp.concatenate([jnp.dot(x_all, gate_half, preferred_element_type=F32).as...  18.3 us
    dot_general x3, matrix products, right_transpose(): lax.dot_general(left, right, (((1,), (1,)), ((), ())), preferred_element_...  16 us
    dot_general x3, matrix products, transpose_product(): lax.dot_general(left, right, (((0,), (0,)), ((), ())), preferred_element_...  14.3 us
    unnamed x1, blocking collectives  14.2 us
    reduce_scatter x1, waiting for transfers between devices, per_device(): lax.psum_scatter(input_part.astype(BF), token_axes, scatter_dimension=0,...  10.1 us
  transfers between devices with their start and end apart: 6, of which 4 were waited for; matrix products, arithmetic and copies ran while one was open for 8% of the time, Pallas kernels for 0%

profile of v1, /device:TPU:0, one launch (start us, length us, event | category | flops | bytes accessed | tf_op | source)
XLA Modules:
  0.0 322.0 jit_solution(10862935364537663238)
XLA Ops:
  7.2 1.0 copy.35
  8.2 1.0 copy.36
  9.3 0.7 convert_bitcast_fusion
  10.0 0.7 pad_maximum_fusion.3
  10.8 0.7 reshape.29
  11.5 2.1 fusion.21
  13.7 28.2 %all-gather.4.cloned.1.call-done = bf16[1024,1152]{0,1:T(8,128)(2,1)} async-done(((bf16[128,1152]{0,1:T(8,128)(2,1)}), bf16[1024,1152]{0,1:T(8,128)(2,1)}) %all-gather.4.cloned.1.call-update) | async-done | bytes 2359312 | tf_op jit(solution)/shard_map/all_gather | solution.py:31
  41.9 1.5 fusion.30
  43.6 5.9 %convolution_convert_fusion = bf16[1024,1792]{1,0:T(8,128)(2,1)} fusion(bf16[3584,512]{1,0:T(8,128)(2,1)} %param.11, s32[]{:T(128)S(6)} %select_n.40, bf16[1024,1152]{0,1:T(8,128)(2,1)} %all-gather.4.cloned.1.call-done), kind=kOutput, calls=%fused_computation | convolution fusion | flops 1880883200 | bytes 6553604 | tf_op jit(solution)/shard_map/dot_general | solution.py:16
  49.6 4.0 %convolution_convert_fusion.1 = bf16[1024,1792]{1,0:T(8,128)(2,1)} fusion(bf16[512,3584]{1,0:T(8,128)(2,1)S(1)} %copy-done.5, s32[]{:T(128)S(6)} %select_n.40, bf16[1024,1152]{0,1:T(8,128)(2,1)S(1)} %copy-done.2), kind=kOutput, calls=%fused_computation.1 | convolution fusion | flops 1880883200 | bytes 6553604 | tf_op jit(solution)/shard_map/dot_general | solution.py:54
  53.5 3.9 %convolution_convert_fusion.2 = bf16[1024,1792]{1,0:T(8,128)(2,1)} fusion(bf16[512,3584]{1,0:T(8,128)(2,1)S(1)} %copy-done.6, s32[]{:T(128)S(6)} %select_n.40, bf16[1024,1152]{0,1:T(8,128)(2,1)S(1)} %copy-done.2), kind=kOutput, calls=%fused_computation.2 | convolution fusion | flops 1880883200 | bytes 6553604 | tf_op jit(solution)/shard_map/dot_general | solution.py:53
  57.6 18.3 %concatenate.19 = bf16[1024,5504]{1,0:T(8,128)(2,1)} concatenate(bf16[1024,1792]{1,0:T(8,128)(2,1)} %convolution_convert_fusion.2, bf16[1024,1792]{1,0:T(8,128)(2,1)} %convolution_convert_fusion.1, bf16[1024,1792]{1,0:T(8,128)(2,1)} %convolution_convert_fusion, bf16[1024,1]{1,0:T(8,128)(2,1)S(1)} %broadcast_in_dim.14, bf16[1024,28]{1,0:T(8,128)(2,1)S(1)} %bitcast.16, ...), dimensions={1} | concatenate | bytes 22544384 | tf_op jit(solution)/shard_map/concatenate | solution.py:51
  76.5 0.6 dynamic-slice.1
  77.8 0.7 dynamic-slice_convert_fusion.2
  78.5 89.8 %reduce-scatter.7.cloned.1.call-done = bf16[64,5504]{1,0:T(8,128)(2,1)} async-done(((bf16[1024,5504]{1,0:T(8,128)(2,1)}), bf16[64,5504]{1,0:T(8,128)(2,1)}) %reduce-scatter.7.cloned.1.call-update) | async-done | bytes 704528
  168.3 2.1 copy.42
  170.4 1.1 copy-done
  171.5 1.5 convert_element_type.91
  173.8 14.2 %all-reduce.2 = f32[512]{0:T(512)S(1)} all-reduce(f32[512]{0:T(512)S(1)} %dynamic-update-slice), channel_id=2, replica_groups=mesh['row'=16,'col'=4,'dp'=2] {'col','dp'}, use_global_device_ids=true, to_apply=%add.2 | all-reduce | flops 512 | bytes 4096
  188.2 0.8 fusion.49
  189.8 1.8 copy.40
  191.9 79.7 %all-gather.6.cloned.1.call-done = bf16[1024,5504]{1,0:T(8,128)(2,1)} async-done(((bf16[64,5504]{1,0:T(8,128)(2,1)}), bf16[1024,5504]{1,0:T(8,128)(2,1)}) %all-gather.6.cloned.1.call-update) | async-done | bytes 11272208 | tf_op jit(solution)/shard_map/all_gather | solution.py:82
  271.6 4.8 %fusion.2 = f32[1024,512]{1,0:T(8,128)S(1)} fusion(bf16[1024,5504]{1,0:T(8,128)(2,1)} %all-gather.6.cloned.1.call-done, bf16[512,3584]{1,0:T(8,128)(2,1)} %param.10, s32[]{:T(128)S(6)} %select_n.40), kind=kOutput, calls=%fused_computation.7 | convolution fusion | flops 1879048192 | bytes 7602180 | tf_op jit(solution)/shard_map/dot_general | solution.py:16
  276.5 5.3 %add_convert_fusion = bf16[1024,512]{1,0:T(8,128)(2,1)} fusion(f32[1024,512]{1,0:T(8,128)S(1)} %fusion.2, bf16[512,3584]{1,0:T(8,128)(2,1)S(1)} %copy-done.7, s32[]{:T(128)S(6)} %select_n.40, bf16[1024,5504]{1,0:T(8,128)(2,1)} %all-gather.6.cloned.1.call-done), kind=kOutput, calls=%fused_computation.19 | convolution fusion | flops 1880096768 | bytes 8650756 | tf_op jit(solution)/shard_map/dot_general | solution.py:16
  281.8 4.1 %fusion.4 = f32[512,1792]{1,0:T(8,128)S(1)} fusion(bf16[1024,5504]{1,0:T(8,128)(2,1)} %all-gather.6.cloned.1.call-done, bf16[1024,1152]{0,1:T(8,128)(2,1)S(1)} %copy-done.3), kind=kOutput, calls=%fused_computation.9 | convolution fusion | flops 1879048192 | bytes 8388608 | tf_op jit(solution)/shard_map/dot_general | solution.py:12
  286.1 4.1 %fusion.8 = f32[512,1792]{1,0:T(8,128)S(1)} fusion(bf16[1024,5504]{1,0:T(8,128)(2,1)} %all-gather.6.cloned.1.call-done, bf16[1024,1152]{0,1:T(8,128)(2,1)S(1)} %copy-done.3), kind=kOutput, calls=%fused_computation.13 | convolution fusion | flops 1879048192 | bytes 8388608 | tf_op jit(solution)/shard_map/dot_general | solution.py:12
  290.9 1.4 convert_add_fusion
  292.4 6.1 %fusion = f32[1792,512]{1,0:T(8,128)} fusion(bf16[1024,5504]{1,0:T(8,128)(2,1)} %all-gather.6.cloned.1.call-done, f32[512]{0:T(512)S(1)} %convert_element_type.107, f32[1024]{0:T(1024)S(1)} %get-tuple-element.9, bf16[1024,1152]{0,1:T(8,128)(2,1)S(1)} %copy-done.3), kind=kOutput, calls=%fused_computation.3 | convolution fusion | flops 1881145344 | bytes 8394752 | tf_op jit(solution)/shard_map/dot_general | solution.py:12
  298.8 2.3 pad_maximum_fusion.1
  301.3 2.3 pad_maximum_fusion
  303.7 10.1 %reduce-scatter.5.cloned.1.call-done = bf16[128,512]{1,0:T(8,128)(2,1)} async-done(((bf16[1024,512]{1,0:T(8,128)(2,1)}), bf16[128,512]{1,0:T(8,128)(2,1)}) %reduce-scatter.5.cloned.1.call-update) | async-done | bytes 131088 | tf_op jit(solution)/shard_map/reduce_scatter | solution.py:92
  313.8 1.7 convert_add_fusion.1
  (55 shorter events, 4.6 us)
Async XLA Ops:
  7.2 34.7 %all-gather.4.cloned.1.call-start = ((), (), s32[]{:S(2)}) async-start(), calls=%async_computation.2 | async-start | bytes 2654208 | tf_op jit(solution)/shard_map/all_gather | solution.py:31
  10.7 157.6 %reduce-scatter.7.cloned.1.call-start = ((), (), s32[]{:S(2)}) async-start(), calls=%async_computation.5 | async-start | bytes 11976704
  43.6 6.0 %copy-start.2 = (bf16[1024,1152]{0,1:T(8,128)(2,1)S(1)}, bf16[1024,1152]{0,1:T(8,128)(2,1)}, u32[]{:S(2)}) copy-start(bf16[1024,1152]{0,1:T(8,128)(2,1)} %all-gather.4.cloned.1.call-done) | copy-start | bytes 7077892
  43.6 5.9 %copy-start.5 = (bf16[512,3584]{1,0:T(8,128)(2,1)S(1)}, bf16[512,3584]{1,0:T(8,128)(2,1)}, u32[]{:S(2)}) copy-start(bf16[512,3584]{1,0:T(8,128)(2,1)} %param.10) | copy-start | bytes 11010052
  49.6 4.0 %copy-start.6 = (bf16[512,3584]{1,0:T(8,128)(2,1)S(1)}, bf16[512,3584]{1,0:T(8,128)(2,1)}, u32[]{:S(2)}) copy-start(bf16[512,3584]{1,0:T(8,128)(2,1)} %param.9) | copy-start | bytes 11010052
  75.9 0.7 copy-start.8
  75.9 1.9 slice-start
  75.9 195.7 %all-gather.6.cloned.1.call-start = ((), (), s32[]{:S(2)}) async-start(), calls=%async_computation.3 | async-start | bytes 11976704 | tf_op jit(solution)/shard_map/all_gather | solution.py:82
  170.4 1.1 copy-start
  189.5 2.4 copy-start.4
  191.6 122.1 %reduce-scatter.5.cloned.1.call-start = ((), (), s32[]{:S(2)}) async-start(), calls=%async_computation.4 | async-start | bytes 1179648 | tf_op jit(solution)/shard_map/reduce_scatter | solution.py:92
  271.6 4.9 %copy-start.7 = (bf16[512,3584]{1,0:T(8,128)(2,1)S(1)}, bf16[512,3584]{1,0:T(8,128)(2,1)}, u32[]{:S(2)}) copy-start(bf16[512,3584]{1,0:T(8,128)(2,1)} %param.9) | copy-start | bytes 11010052
  276.5 5.3 %copy-start.3 = (bf16[1024,1152]{0,1:T(8,128)(2,1)S(1)}, bf16[1024,1152]{0,1:T(8,128)(2,1)}, u32[]{:S(2)}) copy-start(bf16[1024,1152]{0,1:T(8,128)(2,1)} %all-gather.4.cloned.1.call-done) | copy-start | bytes 7077892
  286.0 12.5 %collective-permute-start.1 = (bf16[256,1792]{1,0:T(8,128)(2,1)S(1)}, bf16[256,1792]{1,0:T(8,128)(2,1)S(1)}, u32[]{:S(2)}, u32[]{:S(2)}) collective-permute-start(bf16[256,1792]{1,0:T(8,128)(2,1)S(1)} %dynamic-slice_convert_fusion), channel_id=1, source_target_pairs={{0,1},{1,0},{2,3},{3,2},{4,5},{5,4},{6,7},{7,6},{8,9},{9,8},{10,11... | collective-permute-start | bytes 2752520 | tf_op jit(solution)/shard_map/ppermute | solution.py:104
  290.3 10.8 %collective-permute-start = (bf16[256,1792]{1,0:T(8,128)(2,1)S(1)}, bf16[256,1792]{1,0:T(8,128)(2,1)S(1)}, u32[]{:S(2)}, u32[]{:S(2)}) collective-permute-start(bf16[256,1792]{1,0:T(8,128)(2,1)S(1)} %dynamic-slice_convert_fusion.1), channel_id=1, source_target_pairs={{0,1},{1,0},{2,3},{3,2},{4,5},{5,4},{6,7},{7,6},{8,9},{9,8},{10,11... | collective-permute-start | bytes 2752520 | tf_op jit(solution)/shard_map/ppermute | solution.py:104
  301.3 12.4 %copy-start.1 = (bf16[128,512]{1,0:T(8,128)(2,1)S(1)}, bf16[128,512]{1,0:T(8,128)(2,1)}, u32[]{:S(2)}) copy-start(bf16[128,512]{1,0:T(8,128)(2,1)} %param.13) | copy-start | bytes 393220
Sparse Core Ops, SparseCore 0:
  10.8 31.0 all-gather.3
  76.0 92.2 reduce-scatter.6
  191.7 79.8 all-gather.5
  281.9 31.8 reduce-scatter.4
